TPU v7x, 256 devices: a whole 4x4x8 slice. The times are simulated.
256 devices in a mesh: tm: 4 (over y_hi, core), height: 64 (over y_lo, z, x).
Axes of the slice: x: 4, y: 4 (y_hi: 2, y_lo: 2; y = y_hi * 2 + y_lo), z: 8, core: 2. Of those that a mesh axis runs over, the one named last changes fastest.
Arguments:
- clip: bfloat16 [16, 64, 128, 256], P('tm', 'height'), may hold values from -6 to 6
- conv_weight: bfloat16 [3, 3, 3, 256, 256], replicated, may hold values from -0.078125 to 0.078125
- down_weight: bfloat16 [3, 256, 256], replicated, may hold values from -0.21875 to 0.21875
- grad_out: bfloat16 [8, 64, 128, 256], P('tm', 'height'), may hold values from -6 to 6
Outputs:
- grad_input: bfloat16 [16, 64, 128, 256], P('tm', 'height')
- grad_conv: float32 [6912, 256], P('height', 'tm')
- grad_down: float32 [768, 256], P('height', 'tm')
All inputs are finite; a program needn't handle non-finite values.
Results may differ from a plain program's by a relative error of at most 0.0051.
Values may be sent and summed in bfloat16 or wider, within the bound.
A program may use at most 128 MiB of HBM per device.

v0:
```python
import jax
import jax.numpy as jnp
from jax import lax
from jax.sharding import PartitionSpec as P


def passed_along(value, axis, steps):
    count = lax.axis_size(axis)
    first, last = (max(0, -steps), min(count, count - steps))
    return lax.ppermute(value, axis, [(source, source + steps) for source in range(first, last)])


def padded(block, sides, width):
    for axis, dim in sides:
        count = lax.axis_size(axis)
        forward = [(i, i + 1) for i in range(count - 1)]
        backward = [(target, source) for source, target in forward]
        low = lax.ppermute(
            lax.slice_in_dim(block, block.shape[dim] - width, None, axis=dim), axis, forward
        )
        high = lax.ppermute(lax.slice_in_dim(block, 0, width, axis=dim), axis, backward)
        block = jnp.concatenate([low, block, high], axis=dim)
    return block


def silu_grad(value):
    sig = jax.nn.sigmoid(value)
    return sig * (1.0 + value * (1.0 - sig))


def spread_back(here, later, down_weight):
    chans = here.shape[-1]
    here_flat = here.reshape(-1, chans)
    later_flat = later.reshape(-1, chans)
    even = jnp.dot(later_flat, down_weight[0].T, preferred_element_type=jnp.float32) + jnp.dot(
        here_flat, down_weight[2].T, preferred_element_type=jnp.float32
    )
    odd = jnp.dot(later_flat, down_weight[1].T, preferred_element_type=jnp.float32)
    shape = here.shape
    stacked = jnp.stack([even.reshape(shape), odd.reshape(shape)], axis=1)
    return stacked.reshape((2 * shape[0],) + shape[1:]).astype(jnp.bfloat16)


def clip_edges(rimmed, first_dev, last_dev):
    total = rimmed.shape[1]
    position = jnp.arange(total, dtype=jnp.int32).reshape(1, total, 1, 1)
    drop = jnp.logical_or(
        jnp.logical_and(position == 0, first_dev), jnp.logical_and(position == total - 1, last_dev)
    )
    return jnp.where(drop, jnp.zeros_like(rimmed), rimmed)


def body(clip, conv_weight, down_weight, grad_out):
    nframes, nrows, ncols, chans = clip.shape
    half = grad_out.shape[0]
    cells = nframes * nrows * ncols
    split_count = lax.axis_size("height")
    place = lax.axis_index("height") % split_count
    first_dev = place == 0
    last_dev = place == split_count - 1
    inputs = clip.astype(jnp.float32)
    act = jax.nn.silu(inputs).astype(jnp.bfloat16)
    earlier = passed_along(act[nframes - 2 :], "tm", 1)
    act_ext = jnp.concatenate([earlier, act], axis=0)
    act_rim = padded(act_ext, (("height", 1),), 1)
    act_rim = clip_edges(act_rim, first_dev, last_dev)
    act_pad = jnp.pad(act_rim, ((0, 0), (0, 0), (1, 1), (0, 0)))
    patches = []
    conv = jnp.zeros((cells, chans), jnp.float32)
    for a in range(3):
        for b in range(3):
            patch = jnp.concatenate(
                [act_pad[a : a + nframes, b : b + nrows, c : c + ncols] for c in range(3)], axis=-1
            ).reshape(cells, 3 * chans)
            patches.append(patch)
            conv = conv + jnp.dot(
                patch,
                conv_weight[a, b].reshape(3 * chans, chans),
                preferred_element_type=jnp.float32,
            )
    summed = (inputs + conv.reshape(clip.shape)).astype(jnp.bfloat16)
    prior = passed_along(summed[nframes - 2 :], "tm", 1)
    sum_ext = jnp.concatenate([prior, summed], axis=0)
    following = passed_along(grad_out[:1], "tm", -1)
    later = jnp.concatenate([grad_out[1:], following], axis=0)
    grad_sum = spread_back(grad_out, later, down_weight)
    ahead = passed_along(grad_sum[:2], "tm", -1)
    grad_rim = padded(jnp.concatenate([grad_sum, ahead], axis=0), (("height", 1),), 1)
    grad_rim = clip_edges(grad_rim, first_dev, last_dev)
    out_flat = grad_out.reshape(-1, chans)
    down_terms = []
    for k in range(3):
        picked = sum_ext[k : k + 2 * half : 2].reshape(-1, chans)
        down_terms.append(jnp.dot(picked.T, out_flat, preferred_element_type=jnp.float32))
    term_down = jnp.concatenate(down_terms, axis=0)
    grad_pad = jnp.pad(grad_rim, ((0, 0), (0, 0), (1, 1), (0, 0)))
    grad_flat = grad_sum.reshape(cells, chans)
    grad_act = jnp.zeros((cells, chans), jnp.float32)
    conv_terms = []
    for a in range(3):
        for b in range(3):
            conv_terms.append(
                jnp.dot(patches[a * 3 + b].T, grad_flat, preferred_element_type=jnp.float32)
            )
            back = jnp.concatenate(
                [
                    grad_pad[2 - a : 2 - a + nframes, 2 - b : 2 - b + nrows, 2 - c : 2 - c + ncols]
                    for c in range(3)
                ],
                axis=-1,
            ).reshape(cells, 3 * chans)
            flipped = jnp.transpose(conv_weight[a, b], (0, 2, 1)).reshape(3 * chans, chans)
            grad_act = grad_act + jnp.dot(back, flipped, preferred_element_type=jnp.float32)
    term_conv = jnp.concatenate(conv_terms, axis=0)
    partial_sums = (
        lax.psum_scatter(term_conv, "height", scatter_dimension=0, tiled=True),
        lax.psum_scatter(term_down, "height", scatter_dimension=0, tiled=True),
    )
    grad_conv, grad_down = (
        lax.psum_scatter(partial_sums[0], "tm", scatter_dimension=1, tiled=True),
        lax.psum_scatter(partial_sums[1], "tm", scatter_dimension=1, tiled=True),
    )
    grad_input = (
        grad_sum.astype(jnp.float32) + grad_act.reshape(clip.shape) * silu_grad(inputs)
    ).astype(jnp.bfloat16)
    return (grad_input, grad_conv, grad_down)


def solution(mesh):
    placed = (P("tm", "height", None, None), P(), P(), P("tm", "height", None, None))
    return jax.shard_map(
        body,
        mesh=mesh,
        in_specs=placed,
        out_specs=(P("tm", "height", None, None), P("height", "tm"), P("height", "tm")),
        check_vma=False,
    )
```

profile of v0, /device:TPU:1, one launch (start us, length us, event | category | flops | bytes accessed | tf_op | source)
XLA Modules:
  0.0 494.4 jit_solution(699195529260526452)
XLA Ops:
  8.6 6.2 %collective-permute-start.4 = (bf16[2,1,128,256]{2,3,0,1:T(8,128)(2,1)S(1)}, bf16[2,1,128,256]{2,3,0,1:T(8,128)(2,1)S(1)}, u32[]{:S(2)}, u32[]{:S(2)}) collective-permute-start(bf16[2,1,128,256]{2,3,0,1:T(8,128)(2,1)S(1)} %slice.339), channel_id=1, source_target_pairs={{0,64},{64,128},{128,192},{1,65},{65,129},{129,193},{2,66},{66,130... | collective-permute-start | bytes 393224 | tf_op jit(solution)/shard_map/ppermute | solution.py:10
  17.9 4.9 collective-permute-done
  27.6 4.7 collective-permute-start.5
  34.6 4.8 collective-permute-start.2
  39.4 3.1 fusion.48
  53.7 3.5 pad_slice_fusion.1
  59.1 3.6 pad_slice_fusion.19
  92.0 2.7 pad_maximum_fusion.16
  128.6 2.5 pad_maximum_fusion.7
  155.5 6.3 %collective-permute-start.7 = (bf16[2,1,128,256]{2,3,0,1:T(8,128)(2,1)S(1)}, bf16[2,1,128,256]{2,3,0,1:T(8,128)(2,1)S(1)}, u32[]{:S(2)}, u32[]{:S(2)}) collective-permute-start(bf16[2,1,128,256]{2,3,0,1:T(8,128)(2,1)S(1)} %slice.349), channel_id=1, source_target_pairs={{0,64},{64,128},{128,192},{1,65},{65,129},{129,193},{2,66},{66,130... | collective-permute-start | bytes 393224 | tf_op jit(solution)/shard_map/ppermute | solution.py:10
  164.2 162.9 %fusion.47 = (f32[112,256]{1,0:T(8,128)S(1)}, f32[16,256]{1,0:T(8,128)S(1)}) fusion(f32[6912,256]{1,0:T(8,128)} %fusion.2, f32[768,256]{1,0:T(8,128)S(1)} %pad_maximum_fusion.18), kind=kCustom, calls=%all-reduce-scatter.2 | all-reduce-scatter fusion | flops 2097154 | bytes 7996416
  328.4 18.8 %collective-permute-start.25 = (f32[16,256]{1,0:T(8,128)S(1)}, f32[16,256]{1,0:T(8,128)S(1)}, u32[]{:S(2)}, u32[]{:S(2)}) collective-permute-start(f32[16,256]{1,0:T(8,128)S(1)} %get-tuple-element.18), channel_id=1, source_target_pairs={{0,15},{1,16},{2,17},{3,18},{4,19},{5,20},{6,21},{7,22},{8,23},{9,... | collective-permute-start | bytes 49160
  351.1 2.8 collective-permute-start.21
  353.9 5.2 %collective-permute-start.20 = (f32[16,256]{1,0:T(8,128)S(1)}, f32[16,256]{1,0:T(8,128)S(1)}, u32[]{:S(2)}, u32[]{:S(2)}) collective-permute-start(f32[16,256]{1,0:T(8,128)S(1)} %get-tuple-element.18), channel_id=1, source_target_pairs={{0,10},{1,11},{2,12},{3,13},{4,14},{5,15},{6,16},{7,17},{8,18},{9,... | collective-permute-start | bytes 49160
  359.1 6.1 %collective-permute-start.19 = (f32[16,256]{1,0:T(8,128)S(1)}, f32[16,256]{1,0:T(8,128)S(1)}, u32[]{:S(2)}, u32[]{:S(2)}) collective-permute-start(f32[16,256]{1,0:T(8,128)S(1)} %get-tuple-element.18), channel_id=1, source_target_pairs={{0,9},{1,10},{2,11},{3,12},{4,13},{5,14},{6,15},{7,16},{8,17},{9,1... | collective-permute-start | bytes 49160
  366.7 2.5 collective-permute-start.17
  369.2 3.4 collective-permute-start.16
  374.1 3.7 collective-permute-start.14
  377.8 3.1 collective-permute-start.13
  380.9 4.0 collective-permute-start.12
  386.6 4.0 collective-permute-start.9
  394.1 3.7 collective-permute-start.10
  402.9 50.2 %reduce-scatter.13.cloned.1.call-done = f32[64,12]{1,0:T(8,128)} async-done(((f32[256,12]{1,0:T(8,128)}), f32[64,12]{1,0:T(8,128)}) %reduce-scatter.13.cloned.1.call-update) | async-done | bytes 3088
  454.6 33.0 %reduce-scatter.11.cloned.1.call-done = f32[64,108]{1,0:T(8,128)} async-done(((f32[256,108]{1,0:T(8,128)}), f32[64,108]{1,0:T(8,128)}) %reduce-scatter.11.cloned.1.call-update) | async-done | bytes 27664
  (298 shorter events, 132.5 us)
Async XLA Ops:
  7.2 446.0 %reduce-scatter.13.cloned.1.call-start = ((), (), s32[]{:S(2)}) async-start(), calls=%async_computation.3 | async-start | bytes 163840
  8.6 16.9 %collective-permute-start.4 = (bf16[2,1,128,256]{2,3,0,1:T(8,128)(2,1)S(1)}, bf16[2,1,128,256]{2,3,0,1:T(8,128)(2,1)S(1)}, u32[]{:S(2)}, u32[]{:S(2)}) collective-permute-start(bf16[2,1,128,256]{2,3,0,1:T(8,128)(2,1)S(1)} %slice.339), channel_id=1, source_target_pairs={{0,64},{64,128},{128,192},{1,65},{65,129},{129,193},{2,66},{66,130... | collective-permute-start | bytes 393224 | tf_op jit(solution)/shard_map/ppermute | solution.py:10
  26.3 25.5 %collective-permute-start.6 = (bf16[6,1,128,256]{2,3,0,1:T(8,128)(2,1)}, bf16[6,1,128,256]{2,3,0,1:T(8,128)(2,1)}, u32[]{:S(2)}, u32[]{:S(2)}) collective-permute-start(bf16[6,1,128,256]{2,3,0,1:T(8,128)(2,1)} %pad_maximum_fusion.20), channel_id=1, source_target_pairs={{1,0},{2,1},{3,2},{4,3},{5,4},{6,5},{7,6},{8,7},{9,8},{10,9},{11,1... | collective-permute-start | bytes 1179656 | tf_op jit(solution)/shard_map/ppermute | solution.py:21
  27.6 24.2 %collective-permute-start.5 = (bf16[6,1,128,256]{2,3,0,1:T(8,128)(2,1)}, bf16[6,1,128,256]{2,3,0,1:T(8,128)(2,1)}, u32[]{:S(2)}, u32[]{:S(2)}) collective-permute-start(bf16[6,1,128,256]{2,3,0,1:T(8,128)(2,1)} %pad_maximum_fusion.20), channel_id=1, source_target_pairs={{0,1},{1,2},{2,3},{3,4},{4,5},{5,6},{6,7},{7,8},{8,9},{9,10},{10,1... | collective-permute-start | bytes 1179656 | tf_op jit(solution)/shard_map/ppermute | solution.py:18
  33.3 18.5 %collective-permute-start.3 = (bf16[6,1,128,256]{2,3,0,1:T(8,128)(2,1)}, bf16[6,1,128,256]{2,3,0,1:T(8,128)(2,1)}, u32[]{:S(2)}, u32[]{:S(2)}) collective-permute-start(bf16[6,1,128,256]{2,3,0,1:T(8,128)(2,1)} %pad_maximum_fusion.19), channel_id=1, source_target_pairs={{1,0},{2,1},{3,2},{4,3},{5,4},{6,5},{7,6},{8,7},{9,8},{10,9},{11,1... | collective-permute-start | bytes 1179656 | tf_op jit(solution)/shard_map/ppermute | solution.py:21
  34.6 17.2 %collective-permute-start.2 = (bf16[6,1,128,256]{2,3,0,1:T(8,128)(2,1)}, bf16[6,1,128,256]{2,3,0,1:T(8,128)(2,1)}, u32[]{:S(2)}, u32[]{:S(2)}) collective-permute-start(bf16[6,1,128,256]{2,3,0,1:T(8,128)(2,1)} %pad_maximum_fusion.19), channel_id=1, source_target_pairs={{0,1},{1,2},{2,3},{3,4},{4,5},{5,6},{6,7},{7,8},{8,9},{9,10},{10,1... | collective-permute-start | bytes 1179656 | tf_op jit(solution)/shard_map/ppermute | solution.py:18
  327.1 24.0 %collective-permute-start.26 = (f32[12,256]{1,0:T(8,128)S(1)}, f32[12,256]{1,0:T(8,128)S(1)}, u32[]{:S(2)}, u32[]{:S(2)}) collective-permute-start(f32[12,256]{1,0:T(8,128)S(1)} %slice.351), channel_id=1, source_target_pairs={{0,16},{1,17},{2,18},{3,19},{4,20},{5,21},{6,22},{7,23},{8,24},{9,... | collective-permute-start | bytes 36872
  328.4 25.5 %collective-permute-start.25 = (f32[16,256]{1,0:T(8,128)S(1)}, f32[16,256]{1,0:T(8,128)S(1)}, u32[]{:S(2)}, u32[]{:S(2)}) collective-permute-start(f32[16,256]{1,0:T(8,128)S(1)} %get-tuple-element.18), channel_id=1, source_target_pairs={{0,15},{1,16},{2,17},{3,18},{4,19},{5,20},{6,21},{7,22},{8,23},{9,... | collective-permute-start | bytes 49160
  347.2 11.9 %collective-permute-start.24 = (f32[16,256]{1,0:T(8,128)S(1)}, f32[16,256]{1,0:T(8,128)S(1)}, u32[]{:S(2)}, u32[]{:S(2)}) collective-permute-start(f32[16,256]{1,0:T(8,128)S(1)} %get-tuple-element.18), channel_id=1, source_target_pairs={{0,14},{1,15},{2,16},{3,17},{4,18},{5,19},{6,20},{7,21},{8,22},{9,... | collective-permute-start | bytes 49160
  348.5 16.7 %collective-permute-start.23 = (f32[16,256]{1,0:T(8,128)S(1)}, f32[16,256]{1,0:T(8,128)S(1)}, u32[]{:S(2)}, u32[]{:S(2)}) collective-permute-start(f32[16,256]{1,0:T(8,128)S(1)} %get-tuple-element.18), channel_id=1, source_target_pairs={{0,13},{1,14},{2,15},{3,16},{4,17},{5,18},{6,19},{7,20},{8,21},{9,... | collective-permute-start | bytes 49160
  349.8 17.0 %collective-permute-start.22 = (f32[16,256]{1,0:T(8,128)S(1)}, f32[16,256]{1,0:T(8,128)S(1)}, u32[]{:S(2)}, u32[]{:S(2)}) collective-permute-start(f32[16,256]{1,0:T(8,128)S(1)} %get-tuple-element.18), channel_id=1, source_target_pairs={{0,12},{1,13},{2,14},{3,15},{4,16},{5,17},{6,18},{7,19},{8,20},{9,... | collective-permute-start | bytes 49160
  351.1 18.2 %collective-permute-start.21 = (f32[16,256]{1,0:T(8,128)S(1)}, f32[16,256]{1,0:T(8,128)S(1)}, u32[]{:S(2)}, u32[]{:S(2)}) collective-permute-start(f32[16,256]{1,0:T(8,128)S(1)} %get-tuple-element.18), channel_id=1, source_target_pairs={{0,11},{1,12},{2,13},{3,14},{4,15},{5,16},{6,17},{7,18},{8,19},{9,... | collective-permute-start | bytes 49160
  353.9 18.8 %collective-permute-start.20 = (f32[16,256]{1,0:T(8,128)S(1)}, f32[16,256]{1,0:T(8,128)S(1)}, u32[]{:S(2)}, u32[]{:S(2)}) collective-permute-start(f32[16,256]{1,0:T(8,128)S(1)} %get-tuple-element.18), channel_id=1, source_target_pairs={{0,10},{1,11},{2,12},{3,13},{4,14},{5,15},{6,16},{7,17},{8,18},{9,... | collective-permute-start | bytes 49160
  359.1 15.0 %collective-permute-start.19 = (f32[16,256]{1,0:T(8,128)S(1)}, f32[16,256]{1,0:T(8,128)S(1)}, u32[]{:S(2)}, u32[]{:S(2)}) collective-permute-start(f32[16,256]{1,0:T(8,128)S(1)} %get-tuple-element.18), channel_id=1, source_target_pairs={{0,9},{1,10},{2,11},{3,12},{4,13},{5,14},{6,15},{7,16},{8,17},{9,1... | collective-permute-start | bytes 49160
  365.2 12.6 %collective-permute-start.18 = (f32[16,256]{1,0:T(8,128)S(1)}, f32[16,256]{1,0:T(8,128)S(1)}, u32[]{:S(2)}, u32[]{:S(2)}) collective-permute-start(f32[16,256]{1,0:T(8,128)S(1)} %get-tuple-element.18), channel_id=1, source_target_pairs={{0,8},{1,9},{2,10},{3,11},{4,12},{5,13},{6,14},{7,15},{8,16},{9,17... | collective-permute-start | bytes 49160
  366.7 14.2 %collective-permute-start.17 = (f32[16,256]{1,0:T(8,128)S(1)}, f32[16,256]{1,0:T(8,128)S(1)}, u32[]{:S(2)}, u32[]{:S(2)}) collective-permute-start(f32[16,256]{1,0:T(8,128)S(1)} %get-tuple-element.18), channel_id=1, source_target_pairs={{0,7},{1,8},{2,9},{3,10},{4,11},{5,12},{6,13},{7,14},{8,15},{9,16}... | collective-permute-start | bytes 49160
  369.2 15.7 %collective-permute-start.16 = (f32[16,256]{1,0:T(8,128)S(1)}, f32[16,256]{1,0:T(8,128)S(1)}, u32[]{:S(2)}, u32[]{:S(2)}) collective-permute-start(f32[16,256]{1,0:T(8,128)S(1)} %get-tuple-element.18), channel_id=1, source_target_pairs={{0,6},{1,7},{2,8},{3,9},{4,10},{5,11},{6,12},{7,13},{8,14},{9,15},... | collective-permute-start | bytes 49160
  372.7 13.9 %collective-permute-start.15 = (f32[16,256]{1,0:T(8,128)S(1)}, f32[16,256]{1,0:T(8,128)S(1)}, u32[]{:S(2)}, u32[]{:S(2)}) collective-permute-start(f32[16,256]{1,0:T(8,128)S(1)} %get-tuple-element.18), channel_id=1, source_target_pairs={{0,5},{1,6},{2,7},{3,8},{4,9},{5,10},{6,11},{7,12},{8,13},{9,14},{... | collective-permute-start | bytes 49160
  374.1 16.5 %collective-permute-start.14 = (f32[16,256]{1,0:T(8,128)S(1)}, f32[16,256]{1,0:T(8,128)S(1)}, u32[]{:S(2)}, u32[]{:S(2)}) collective-permute-start(f32[16,256]{1,0:T(8,128)S(1)} %get-tuple-element.18), channel_id=1, source_target_pairs={{0,4},{1,5},{2,6},{3,7},{4,8},{5,9},{6,10},{7,11},{8,12},{9,13},{1... | collective-permute-start | bytes 49160
  377.8 16.3 %collective-permute-start.13 = (f32[16,256]{1,0:T(8,128)S(1)}, f32[16,256]{1,0:T(8,128)S(1)}, u32[]{:S(2)}, u32[]{:S(2)}) collective-permute-start(f32[16,256]{1,0:T(8,128)S(1)} %get-tuple-element.18), channel_id=1, source_target_pairs={{0,3},{1,4},{2,5},{3,6},{4,7},{5,8},{6,9},{7,10},{8,11},{9,12},{10... | collective-permute-start | bytes 49160
  380.9 16.9 %collective-permute-start.12 = (f32[16,256]{1,0:T(8,128)S(1)}, f32[16,256]{1,0:T(8,128)S(1)}, u32[]{:S(2)}, u32[]{:S(2)}) collective-permute-start(f32[16,256]{1,0:T(8,128)S(1)} %get-tuple-element.18), channel_id=1, source_target_pairs={{0,2},{1,3},{2,4},{3,5},{4,6},{5,7},{6,8},{7,9},{8,10},{9,11},{10,... | collective-permute-start | bytes 49160
  385.0 12.9 %collective-permute-start.11 = (f32[16,256]{1,0:T(8,128)S(1)}, f32[16,256]{1,0:T(8,128)S(1)}, u32[]{:S(2)}, u32[]{:S(2)}) collective-permute-start(f32[16,256]{1,0:T(8,128)S(1)} %get-tuple-element.18), channel_id=1, source_target_pairs={{0,1},{1,2},{2,3},{3,4},{4,5},{5,6},{6,7},{7,8},{8,9},{9,10},{10,1... | collective-permute-start | bytes 49160
  386.6 14.0 %collective-permute-start.9 = (f32[112,256]{1,0:T(8,128)S(1)}, f32[112,256]{1,0:T(8,128)S(1)}, u32[]{:S(2)}, u32[]{:S(2)}) collective-permute-start(f32[112,256]{1,0:T(8,128)S(1)} %get-tuple-element.17), channel_id=1, source_target_pairs={{0,2},{1,3},{2,4},{3,5},{4,6},{5,7},{6,8},{7,9},{8,10},{9,11},{10,... | collective-permute-start | bytes 344072
  400.5 87.1 %reduce-scatter.11.cloned.1.call-start = ((), (), s32[]{:S(2)}) async-start(), calls=%async_computation.2 | async-start | bytes 163840
  (80 other events, 468.8 us)
Sparse Core Ops, SparseCore 0:
  400.7 52.4 reduce-scatter.12
  456.4 31.1 reduce-scatter.10
where the time goes:
time: 497 us; the launch traced here: 494 us
  blocking collectives  163 us (33%)
  starting transfers between devices  97.7 us (20%)
  waiting for transfers between devices  88.6 us (18%)
  local copies, waits for them, and re-layouts  74.6 us (15%)
  other arithmetic  31.4 us (6%)
  matrix products  23 us (5%)
  between operations  16.3 us (3%)
    unnamed x1, blocking collectives  163 us
    unnamed x23, waiting for transfers between devices  83.3 us
    unnamed x21, starting transfers between devices  69.3 us
    unnamed x171, local copies, waits for them, and re-layouts  24.5 us
    concatenate x9, local copies, waits for them, and re-layouts, body(): jnp.concatenate([act_pad[a:a + nframes, b:b + nrows, c:c + ncols] for c i...  20.7 us
    ppermute x4, starting transfers between devices, passed_along(): lax.ppermute(value, axis, [(source, source + steps) for source in range(f...  16.3 us
    concatenate x8, other arithmetic, body(): jnp.concatenate([act_pad[a:a + nframes, b:b + nrows, c:c + ncols] for c i...  15.9 us
    concatenate x9, local copies, waits for them, and re-layouts, body(): jnp.concatenate([grad_pad[2 - a:2 - a + nframes, 2 - b:2 - b + nrows, 2 -...  14.8 us
  transfers between devices with their start and end apart: 29, of which 4 were waited for; matrix products, arithmetic and copies ran while one was open for 5% of the time, Pallas kernels for 0%

commit v1 on v0

v1 whole, which is shorter than its diff:
```python
import jax
import jax.numpy as jnp
from jax import lax
from jax.experimental import pallas as pl
from jax.experimental.pallas import tpu as pltpu
from jax.sharding import PartitionSpec as P

MESH = pl.DeviceIdType.MESH
F32 = jnp.float32
BF16 = jnp.bfloat16
COLS = 128
CH = 256
SIZES = (112, 112, 112, 112, 64)
DOWN = 4
TAPS = (((0, 4), (13, 17)), ((4, 7), (17, 21)), ((7, 11), (21, 24)), ((11, 13), (24, 27)))


def nt(lhs, rhs):
    return lax.dot_general(lhs, rhs, (((1,), (1,)), ((), ())), preferred_element_type=F32)


def nn(lhs, rhs):
    return jnp.dot(lhs, rhs, preferred_element_type=F32)


def sigmoid(value):
    return 1.0 / (1.0 + jnp.exp(-value))


def shifted(value, row):
    before = jnp.where(row == 0, 0.0, pltpu.roll(value, 1, 0))
    after = jnp.where(row == COLS - 1, 0.0, pltpu.roll(value, COLS - 1, 0))
    return before, after


def kernel(clip, weight, down, gout, g_in, g_conv, g_down, *scratch):
    scratch = list(scratch)
    take = lambda n: [scratch.pop(0) for _ in range(n)]
    (wgt, dwn, cl, go, acts, act_t, gs, cb, acc, part, part_d) = take(11)
    (zt, ztd, zr, zrd) = take(4)
    bufs = [take(9) for _ in SIZES]
    (loc_sem, halo_s, halo_r, red_s, red_r, zs, zsd, zrs, zrds) = take(9)

    tm = lax.axis_index("tm")
    h = lax.axis_index("height")
    core = lax.rem(tm, 2)
    yh = lax.div(tm, 2)
    x = lax.rem(h, 4)
    z = lax.rem(lax.div(h, 4), 8)
    yl = lax.div(h, 32)
    y = yh * 2 + yl

    def dev(xx, yy, zz, cc):
        return (lax.div(yy, 2) * 2 + cc, lax.rem(yy, 2) * 32 + zz * 4 + xx)

    def near(dt, dh):
        return (lax.rem(tm + dt + 4, 4), lax.rem(h + dh + 64, 64))

    def first(d):
        return dev(lax.rem(x + (1 - core) * d, 4), lax.rem(y + core * d, 4), z, core)

    def second(d):
        return dev(lax.rem(x + core * d, 4), lax.rem(y + (1 - core) * d, 4), z, core)

    def remote(src, dst, send, recv, device):
        return pltpu.make_async_remote_copy(
            src_ref=src, dst_ref=dst, send_sem=send, recv_sem=recv, device_id=device, device_id_type=MESH
        )

    barrier = pltpu.get_barrier_semaphore()
    peers = [near(dt, dh) for dt in (-1, 1) for dh in (-1, 0, 1)] + [near(0, -1), near(0, 1)]
    peers += [first(d) for d in (1, 2, 3)] + [second(d) for d in (1, 2, 3)]
    peers += [dev(x, y, lax.rem(z + d, 8), c) for d in range(1, 8) for c in (0, 1)]
    for peer in peers:
        pl.semaphore_signal(barrier, inc=1, device_id=peer, device_id_type=MESH)

    loads = [
        pltpu.make_async_copy(clip.at[:, 0], cl.at[pl.ds(2, 4)], loc_sem.at[0]),
        pltpu.make_async_copy(gout.at[:, 0], go.at[1, pl.ds(0, 2)], loc_sem.at[1]),
        pltpu.make_async_copy(down, dwn, loc_sem.at[2]),
    ] + [pltpu.make_async_copy(weight.at[a], wgt.at[a], loc_sem.at[3 + a]) for a in range(3)]
    for load in loads:
        load.start()

    pl.semaphore_wait(barrier, len(peers))

    halo = [
        (gout.at[:, 0], go.at[0, pl.ds(0, 2)], near(0, 1), h < 63, h > 0),
        (gout.at[:, 0], go.at[2, pl.ds(0, 2)], near(0, -1), h > 0, h < 63),
        (gout.at[:, 0], go.at[0, pl.ds(2, 2)], near(-1, 1), (tm > 0) & (h < 63), (tm < 3) & (h > 0)),
        (gout.at[:, 0], go.at[2, pl.ds(2, 2)], near(-1, -1), (tm > 0) & (h > 0), (tm < 3) & (h < 63)),
        (gout.at[:, 0], go.at[1, pl.ds(2, 2)], near(-1, 0), tm > 0, tm < 3),
        (clip.at[pl.ds(2, 2), 0], cl.at[pl.ds(0, 2)], near(1, 0), tm < 3, tm > 0),
    ]
    copies = [remote(s, d, halo_s.at[i], halo_r.at[i], to) for i, (s, d, to, _, _) in enumerate(halo)]

    def when_start(i):
        @pl.when(halo[i][3])
        def _():
            copies[i].start()

    def when_recv(i):
        @pl.when(halo[i][4])
        def _():
            copies[i].wait_recv()

        @pl.when(jnp.logical_not(halo[i][4]))
        def _():
            dst = halo[i][1]
            dst[...] = jnp.zeros(dst.shape, BF16)

    for i in (5, 0, 1, 4, 2, 3):
        when_start(i)

    row = lax.broadcasted_iota(jnp.int32, (COLS, CH), 0)

    def act_frame(f, carry):
        value = cl[f].astype(F32)
        act = value * sigmoid(value)
        before, after = shifted(act, row)
        acts[0, f] = before.astype(BF16)
        acts[1, f] = act.astype(BF16)
        acts[2, f] = after.astype(BF16)
        return carry

    loads[0].wait()
    lax.fori_loop(2, 6, act_frame, 0)
    act_t[...] = acts[1, pl.ds(2, 4)].reshape(4 * COLS, CH).T
    when_recv(5)
    lax.fori_loop(0, 2, act_frame, 0)
    for a in range(3):
        loads[3 + a].wait()

    def conv_rows(b, carry):
        total = jnp.zeros((4 * COLS, CH), F32)
        for a in range(3):
            lhs = jnp.concatenate([acts[c, pl.ds(a, 4)].reshape(4 * COLS, CH) for c in range(3)], axis=1)
            total = total + nn(lhs, wgt[a, b].reshape(3 * CH, CH))
        own = cl[pl.ds(2, 4)].reshape(4 * COLS, CH).astype(F32)
        total = total + jnp.where(b == 1, own, 0.0)
        cb[b] = total.astype(BF16).reshape(4, COLS, CH)
        return carry

    lax.fori_loop(0, 3, conv_rows, 0)

    loads[1].wait()
    loads[2].wait()
    for i in range(5):
        when_recv(i)

    def grad_rows(r, carry):
        later = go[r, pl.ds(1, 3)].reshape(3 * COLS, CH)
        here = go[r, pl.ds(0, 3)].reshape(3 * COLS, CH)
        even = nt(later, dwn[0]) + nt(here, dwn[2])
        odd = nt(later, dwn[1])
        for v in range(3):
            for k, whole in ((0, even), (1, odd)):
                value = whole[v * COLS : (v + 1) * COLS]
                before, after = shifted(value, row)
                gs[0, r, 2 * v + k] = after.astype(BF16)
                gs[1, r, 2 * v + k] = value.astype(BF16)
                gs[2, r, 2 * v + k] = before.astype(BF16)
        return carry

    lax.fori_loop(0, 3, grad_rows, 0)

    for k, pairs in ((0, ((0, 1), (2, 2))), (1, ((1, 1), (3, 2))), (2, ((0, 0), (2, 1)))):
        lhs = jnp.concatenate([cb[b, t] for b in range(3) for t, _ in pairs], axis=0)
        rhs = jnp.concatenate([go[2 - b, u] for b in range(3) for _, u in pairs], axis=0)
        part_d[k * CH : (k + 1) * CH, :] = lax.dot_general(
            lhs, rhs, (((0,), (0,)), ((), ())), preferred_element_type=F32
        )

    def taps(c):
        def one(t, carry):
            a, b, s = lax.div(t, 9), lax.rem(lax.div(t, 3), 3), lax.rem(t, 3)
            rhs = gs[s, 2 - b, pl.ds(2 - a, 4)].reshape(4 * COLS, CH)
            part[pl.ds(pl.multiple_of(t * CH, CH), CH), :] = nn(act_t[...], rhs)
            return carry

        for lo, hi in TAPS[c]:
            lax.fori_loop(lo, hi, one, 0)

    def blocks(c, cc, put):
        def two(i, carry):
            l, pair = lax.div(i, 2), lax.rem(i, 2)
            if c == DOWN:
                for j in range(4):
                    base = pl.multiple_of(24 * (16 * l + 2 * (2 * j + cc) + pair), 8)
                    each(part_d, base, 16, 8, slice(16 * j, 16 * j + 16), l, pair)
            else:
                base = pl.multiple_of(216 * (16 * l + 2 * (2 * c + cc) + pair), 8)
                each(part, base, 112, 104, slice(0, 112), l, pair)
            return carry

        def each(src, base, size, skip, where, l, pair):
            for odd in range(2):
                value = src[pl.ds(base + skip * odd, size), :]
                xx = 2 * pair + odd
                for hi in range(2):
                    yy = 2 * hi + l
                    p = (1 - cc) * xx + cc * yy
                    q = (1 - cc) * yy + cc * xx
                    put(p, q, where, value[:, 128 * hi : 128 * hi + 128])

        lax.fori_loop(0, 4, two, 0)

    partner = dev(x, y, z, 1 - core)
    p0 = (1 - core) * x + core * y
    q0 = (1 - core) * y + core * x
    pn, pp, po = lax.rem(p0 + 1, 4), lax.rem(p0 + 3, 4), lax.rem(p0 + 2, 4)

    def message(c, i):
        s_, sr, b_, leg, dr, cs, cm, r_, rx = bufs[c]
        lo, hi = pl.ds(0, 2), pl.ds(2, 2)
        if i == 0:
            src, dst, to = s_, sr, partner
        elif i == 1:
            src, dst, to = b_.at[po, lo], leg.at[0], first(1)
        elif i == 2:
            src, dst, to = b_.at[po, hi], leg.at[1], first(3)
        elif i == 3:
            src, dst, to = b_.at[pn, hi], dr.at[0], first(1)
        elif i == 4:
            src, dst, to = b_.at[pp, lo], dr.at[1], first(3)
        elif i == 5:
            src, dst, to = cs.at[0], cm.at[0], first(1)
        elif i == 6:
            src, dst, to = cs.at[1], cm.at[1], first(3)
        else:
            d = i - 6
            src, dst, to = r_.at[lax.rem(q0 + d, 4)], rx.at[d - 1], second(d)
        return remote(src, dst, red_s.at[c, i], red_r.at[c, i], to)

    def hand_over(c):
        s_ = bufs[c][0]

        def put(p, q, where, value):
            s_[p, q, where] = value.astype(BF16)

        blocks(c, 1 - core, put)
        message(c, 0).start()

    def combine(c):
        sr, b_ = bufs[c][1], bufs[c][2]
        message(c, 0).wait_recv()

        def put(p, q, where, value):
            b_[p, q, where] = (value + sr[p, q, where].astype(F32)).astype(BF16)

        blocks(c, core, put)
        for i in (1, 2, 3, 4):
            message(c, i).start()

    def relay(c):
        _, _, b_, leg, _, cs, _, _, _ = bufs[c]
        message(c, 1).wait_recv()
        cs[0] = (b_[pn, pl.ds(0, 2)].astype(F32) + leg[0].astype(F32)).astype(BF16)
        message(c, 5).start()
        message(c, 2).wait_recv()
        cs[1] = (b_[pp, pl.ds(2, 2)].astype(F32) + leg[1].astype(F32)).astype(BF16)
        message(c, 6).start()

    def turn(c):
        _, _, b_, _, dr, _, cm, r_, _ = bufs[c]
        for i in (3, 4, 5, 6):
            message(c, i).wait_recv()
        for half in range(2):
            both = pl.ds(2 * half, 2)
            total = b_[p0, both].astype(F32) + cm[half].astype(F32) + dr[1 - half].astype(F32)
            r_[both] = total.astype(BF16)
        for i in (7, 8, 9):
            message(c, i).start()

    lane = lax.broadcasted_iota(jnp.int32, (64, 128), 1)

    def z_send(src, dst, keep, send, recv, to_z, k):
        own = (to_z == z) & (core == k)

        @pl.when(own)
        def _():
            dst.at[z][...] = src[...]

        @pl.when(jnp.logical_not(own))
        def _():
            remote(src, dst.at[z], send, recv.at[z], dev(x, y, to_z, k)).start()

    def z_wait(src, dst, send, recv, to_z, k):
        @pl.when(jnp.logical_not((to_z == z) & (core == k)))
        def _():
            remote(src, dst.at[z], send, recv.at[z], dev(x, y, to_z, k)).wait_send()

    def leave(c):
        r_, rx = bufs[c][7], bufs[c][8]
        for i in (7, 8, 9):
            message(c, i).wait_recv()
        total = r_[q0].astype(F32)
        for d in range(3):
            total = total + rx[d].astype(F32)
        if c == DOWN:
            ztd[...] = total.astype(BF16).reshape(4, 16, 128)
            for j in range(4):
                for k in range(2):
                    z_send(ztd.at[j], zrd, None, zsd.at[j, k], zrds, 2 * j + core, k)
        else:
            top, low = total[0:64], total[48:112]
            zt[c, 0] = jnp.where(lane < 64, top, pltpu.roll(low, 64, 1)).astype(BF16)
            zt[c, 1] = jnp.where(lane < 64, pltpu.roll(top, 64, 1), low).astype(BF16)
            for k in range(2):
                z_send(zt.at[c, k], zr, None, zs.at[c, k], zrs, 2 * c + core, k)

    def grad_act(b):
        def one(a, carry):
            total = acc[...]
            for s in range(3):
                total = total + nt(gs[s, 2 - b, pl.ds(2 - a, 4)].reshape(4 * COLS, CH), wgt[a, b, s])
            acc[...] = total
            return carry

        lax.fori_loop(0, 3, one, 0)

    acc[...] = jnp.zeros(acc.shape, F32)
    hand_over(DOWN)
    taps(0)
    hand_over(0)
    combine(DOWN)
    taps(1)
    hand_over(1)
    combine(0)
    relay(DOWN)
    taps(2)
    hand_over(2)
    combine(1)
    relay(0)
    turn(DOWN)
    taps(3)
    hand_over(3)
    combine(2)
    relay(1)
    turn(0)
    combine(3)
    leave(DOWN)
    grad_act(0)
    relay(2)
    turn(1)
    leave(0)
    grad_act(1)
    relay(3)
    turn(2)
    leave(1)
    grad_act(2)

    def finish(f, carry):
        value = cl[f + 2].astype(F32)
        sig = sigmoid(value)
        grad = acc[pl.ds(pl.multiple_of(f * COLS, COLS), COLS), :]
        g_in[f, 0] = (gs[1, 1, f].astype(F32) + grad * (sig * (1.0 + value * (1.0 - sig)))).astype(BF16)
        return carry

    lax.fori_loop(0, 4, finish, 0)
    turn(3)
    leave(2)
    leave(3)

    mine = lax.rem(z, 2)
    for s in range(8):
        @pl.when(jnp.logical_not((z == s) & (core == mine)))
        def _():
            remote(ztd.at[0], zrd.at[s], zsd.at[0, 0], zrds.at[s], partner).wait_recv()
            remote(zt.at[0, 0], zr.at[s], zs.at[0, 0], zrs.at[s], partner).wait_recv()

    x_odd = lax.rem(x, 2) == 1
    total = zr[0].astype(F32)
    total_d = zrd[0].astype(F32)
    for s in range(1, 8):
        total = total + zr[s].astype(F32)
        total_d = total_d + zrd[s].astype(F32)
    whole = jnp.concatenate([total, pltpu.roll(total, 64, 1)[16:64]], axis=0)
    whole = jnp.where(x_odd, pltpu.roll(whole, 108, 0), whole)
    g_conv[...] = whole[0:108, 0:64]
    total_d = jnp.where(core == 1, pltpu.roll(total_d, 64, 1), total_d)
    total_d = jnp.where(x_odd, pltpu.roll(total_d, 12, 0), total_d)
    g_down[...] = total_d[0:12, 0:64]

    for i in range(6):
        @pl.when(halo[i][3])
        def _():
            copies[i].wait_send()

    for c in range(5):
        for i in range(10):
            message(c, i).wait_send()
    for c in range(4):
        for k in range(2):
            z_wait(zt.at[c, k], zr, zs.at[c, k], zrs, 2 * c + core, k)
            z_wait(ztd.at[c], zrd, zsd.at[c, k], zrds, 2 * c + core, k)


def body(clip, weight, down, gout):
    vmem = pltpu.VMEM
    chunk = []
    for n in SIZES:
        full, pair = (4, 4, n, 128), (2, 2, n, 128)
        chunk += [vmem(s, BF16) for s in (full, full, full, pair, pair, pair, pair, (4, n, 128), (3, n, 128))]
    dma = pltpu.SemaphoreType.DMA
    scratch = [
        vmem((3, 3, 3, CH, CH), BF16),
        vmem((3, CH, CH), BF16),
        vmem((6, COLS, CH), BF16),
        vmem((3, 4, COLS, CH), BF16),
        vmem((3, 6, COLS, CH), BF16),
        vmem((CH, 4 * COLS), BF16),
        vmem((3, 3, 6, COLS, CH), BF16),
        vmem((3, 4, COLS, CH), BF16),
        vmem((4 * COLS, CH), F32),
        vmem((27 * CH, CH), F32),
        vmem((3 * CH, CH), F32),
        vmem((4, 2, 64, 128), BF16),
        vmem((4, 16, 128), BF16),
        vmem((8, 64, 128), BF16),
        vmem((8, 16, 128), BF16),
        *chunk,
        dma((6,)),
        dma((6,)),
        dma((6,)),
        dma((5, 10)),
        dma((5, 10)),
        dma((4, 2)),
        dma((4, 2)),
        dma((8,)),
        dma((8,)),
    ]
    return pl.pallas_call(
        kernel,
        out_shape=(
            jax.ShapeDtypeStruct(clip.shape, BF16),
            jax.ShapeDtypeStruct((108, 64), F32),
            jax.ShapeDtypeStruct((12, 64), F32),
        ),
        in_specs=[pl.BlockSpec(memory_space=pl.ANY)] * 4,
        out_specs=[pl.BlockSpec(memory_space=vmem)] * 3,
        scratch_shapes=scratch,
        compiler_params=pltpu.CompilerParams(collective_id=0, has_side_effects=True),
        name="block_backward",
    )(clip, weight, down, gout)


def solution(mesh):
    placed = (P("tm", "height", None, None), P(), P(), P("tm", "height", None, None))
    return jax.shard_map(
        body,
        mesh=mesh,
        in_specs=placed,
        out_specs=(P("tm", "height", None, None), P("height", "tm"), P("height", "tm")),
        check_vma=False,
    )
```

time: 497 us -> 56.7 us (0.11)
  the two profiles are of different devices: /device:TPU:1 before, /device:TPU:4 now
where the time goes in v1:
time: 56.7 us; the launch traced here: 56.5 us
  Pallas kernels  51.4 us (91%)
  local copies, waits for them, and re-layouts  4.48 us (8%)
  between operations  0.64 us (1%)
    pallas_call x1, Pallas kernels, body(): pl.pallas_call(kernel, out_shape=(jax.ShapeDtypeStruct(clip.shape, BF16),...  51.4 us
    unnamed x2, local copies, waits for them, and re-layouts  2.96 us
    pallas_call x1, local copies, waits for them, and re-layouts, body(): pl.pallas_call(kernel, out_shape=(jax.ShapeDtypeStruct(clip.shape, BF16),...  1.52 us

profile of v1, /device:TPU:4, one launch (start us, length us, event | category | flops | bytes accessed | tf_op | source)
XLA Modules:
  0.0 56.5 jit_solution(1258313056563683966)
XLA Ops:
  0.6 51.4 %block_backward.1 = (bf16[4,1,128,256]{3,2,1,0:T(8,128)(2,1)}, f32[108,64]{1,0:T(8,128)}, f32[12,64]{1,0:T(8,128)}) custom-call(bf16[4,1,128,256]{3,2,1,0:T(8,128)(2,1)} %clip.1, bf16[3,3,3,256,256]{4,3,2,1,0:T(8,128)(2,1)} %weight.1, bf16[3,256,256]{2,1,0:T(8,128)(2,1)} %down.1, bf16[2,1,128,256]{3,2,1,0:T(8,128)(2,1)} %gout.1), custom_call_target="tpu_custom_call" | custom-call | tf_op jit(solution)/shard_map/block_backward/pallas_call | solution.py:433
  52.0 1.5 %copy.7 = f32[108,64]{0,1:T(8,128)} copy(f32[108,64]{1,0:T(8,128)} %get-tuple-element.4) | data formatting | bytes 55296 | tf_op jit(solution)/shard_map/block_backward/pallas_call | solution.py:433
  53.5 1.7 %copy.10 = bf16[4,1,128,256]{3,2,1,0:T(8,128)(2,1)} copy(bf16[4,1,128,256]{3,2,1,0:T(8,128)(2,1)} %get-tuple-element.9) | data formatting | bytes 524288
  55.2 1.3 %copy.11 = f32[12,64]{1,0:T(8,128)} copy(f32[12,64]{1,0:T(8,128)} %get-tuple-element.11) | data formatting | bytes 6144

commit v2 on v1

--- a/solution.py
+++ b/solution.py
@@ -12,7 +12,8 @@
 CH = 256
 SIZES = (112, 112, 112, 112, 64)
 DOWN = 4
-TAPS = (((0, 4), (13, 17)), ((4, 7), (17, 21)), ((7, 11), (21, 24)), ((11, 13), (24, 27)))
+OWN_ROW = (1, 3, 3)
+TAPS = ((0, 5, 2), (2, 4, 2), (3, 0, 1), (8, 0, 1))
 
 
 def nt(lhs, rhs):
@@ -33,10 +34,10 @@
     return before, after
 
 
-def kernel(clip, weight, down, gout, g_in, g_conv, g_down, *scratch):
+def kernel(clip, weight, down, gout, g_in, sums, *scratch):
     scratch = list(scratch)
     take = lambda n: [scratch.pop(0) for _ in range(n)]
-    (wgt, dwn, cl, go, acts, act_t, gs, cb, acc, part, part_d) = take(11)
+    (wgt, dwn, cl, go, acts, act_t, gs, cb, acc, part, part_d, held) = take(12)
     (zt, ztd, zr, zrd) = take(4)
     bufs = [take(9) for _ in SIZES]
     (loc_sem, halo_s, halo_r, red_s, red_r, zs, zsd, zrs, zrds) = take(9)
@@ -143,12 +144,7 @@
 
     lax.fori_loop(0, 3, conv_rows, 0)
 
-    loads[1].wait()
-    loads[2].wait()
-    for i in range(5):
-        when_recv(i)
-
-    def grad_rows(r, carry):
+    def grad_rows(r):
         later = go[r, pl.ds(1, 3)].reshape(3 * COLS, CH)
         here = go[r, pl.ds(0, 3)].reshape(3 * COLS, CH)
         even = nt(later, dwn[0]) + nt(here, dwn[2])
@@ -160,26 +156,25 @@
                 gs[0, r, 2 * v + k] = after.astype(BF16)
                 gs[1, r, 2 * v + k] = value.astype(BF16)
                 gs[2, r, 2 * v + k] = before.astype(BF16)
-        return carry
-
-    lax.fori_loop(0, 3, grad_rows, 0)
-
-    for k, pairs in ((0, ((0, 1), (2, 2))), (1, ((1, 1), (3, 2))), (2, ((0, 0), (2, 1)))):
-        lhs = jnp.concatenate([cb[b, t] for b in range(3) for t, _ in pairs], axis=0)
-        rhs = jnp.concatenate([go[2 - b, u] for b in range(3) for _, u in pairs], axis=0)
-        part_d[k * CH : (k + 1) * CH, :] = lax.dot_general(
-            lhs, rhs, (((0,), (0,)), ((), ())), preferred_element_type=F32
-        )
-
-    def taps(c):
-        def one(t, carry):
-            a, b, s = lax.div(t, 9), lax.rem(lax.div(t, 3), 3), lax.rem(t, 3)
-            rhs = gs[s, 2 - b, pl.ds(2 - a, 4)].reshape(4 * COLS, CH)
-            part[pl.ds(pl.multiple_of(t * CH, CH), CH), :] = nn(act_t[...], rhs)
+
+    def down_terms():
+        for k, pairs in ((0, ((0, 1), (2, 2))), (1, ((1, 1), (3, 2))), (2, ((0, 0), (2, 1)))):
+            lhs = jnp.concatenate([cb[b, t] for b in range(3) for t, _ in pairs], axis=0)
+            rhs = jnp.concatenate([go[2 - b, u] for b in range(3) for _, u in pairs], axis=0)
+            part_d[k * CH : (k + 1) * CH, :] = lax.dot_general(
+                lhs, rhs, (((0,), (0,)), ((), ())), preferred_element_type=F32
+            )
+
+    def taps(start, step, count):
+        def one(i, carry):
+            ab = start + step * i
+            a, b = lax.div(ab, 3), lax.rem(ab, 3)
+            for s in range(3):
+                rhs = gs[s, 2 - b, pl.ds(2 - a, 4)].reshape(4 * COLS, CH)
+                part[pl.ds(pl.multiple_of((3 * ab + s) * CH, CH), CH), :] = nn(act_t[...], rhs)
             return carry
 
-        for lo, hi in TAPS[c]:
-            lax.fori_loop(lo, hi, one, 0)
+        lax.fori_loop(0, count, one, 0)
 
     def blocks(c, cc, put):
         def two(i, carry):
@@ -268,7 +263,7 @@
         for half in range(2):
             both = pl.ds(2 * half, 2)
             total = b_[p0, both].astype(F32) + cm[half].astype(F32) + dr[1 - half].astype(F32)
-            r_[both] = total.astype(BF16)
+            r_[both] = total.astype(r_.dtype)
         for i in (7, 8, 9):
             message(c, i).start()
 
@@ -298,7 +293,7 @@
         for d in range(3):
             total = total + rx[d].astype(F32)
         if c == DOWN:
-            ztd[...] = total.astype(BF16).reshape(4, 16, 128)
+            ztd[...] = total.reshape(4, 16, 128)
             for j in range(4):
                 for k in range(2):
                     z_send(ztd.at[j], zrd, None, zsd.at[j, k], zrds, 2 * j + core, k)
@@ -309,58 +304,60 @@
             for k in range(2):
                 z_send(zt.at[c, k], zr, None, zs.at[c, k], zrs, 2 * c + core, k)
 
-    def grad_act(b):
-        def one(a, carry):
-            total = acc[...]
+    def grad_act(b, total):
+        for a in range(3):
             for s in range(3):
                 total = total + nt(gs[s, 2 - b, pl.ds(2 - a, 4)].reshape(4 * COLS, CH), wgt[a, b, s])
-            acc[...] = total
-            return carry
-
-        lax.fori_loop(0, 3, one, 0)
-
-    acc[...] = jnp.zeros(acc.shape, F32)
-    hand_over(DOWN)
-    taps(0)
-    hand_over(0)
-    combine(DOWN)
-    taps(1)
-    hand_over(1)
-    combine(0)
-    relay(DOWN)
-    taps(2)
-    hand_over(2)
-    combine(1)
-    relay(0)
-    turn(DOWN)
-    taps(3)
-    hand_over(3)
-    combine(2)
-    relay(1)
-    turn(0)
-    combine(3)
-    leave(DOWN)
-    grad_act(0)
-    relay(2)
-    turn(1)
-    leave(0)
-    grad_act(1)
-    relay(3)
-    turn(2)
-    leave(1)
-    grad_act(2)
+        return total
 
     def finish(f, carry):
         value = cl[f + 2].astype(F32)
         sig = sigmoid(value)
         grad = acc[pl.ds(pl.multiple_of(f * COLS, COLS), COLS), :]
-        g_in[f, 0] = (gs[1, 1, f].astype(F32) + grad * (sig * (1.0 + value * (1.0 - sig)))).astype(BF16)
+        held[f, 0] = (gs[1, 1, f].astype(F32) + grad * (sig * (1.0 + value * (1.0 - sig)))).astype(BF16)
         return carry
 
+    loads[1].wait()
+    loads[2].wait()
+    when_recv(4)
+    grad_rows(1)
+    taps(*OWN_ROW)
+    acc[...] = grad_act(1, jnp.zeros(acc.shape, F32))
+
+    for i in range(4):
+        when_recv(i)
+    grad_rows(0)
+    grad_rows(2)
+    for c in range(4):
+        taps(*TAPS[c])
+        hand_over(c)
+    combine(0)
+    down_terms()
+    hand_over(DOWN)
+    combine(1)
+    acc[...] = grad_act(0, acc[...])
+    relay(0)
+    combine(2)
+    acc[...] = grad_act(2, acc[...])
+    relay(1)
+    combine(3)
+    turn(0)
     lax.fori_loop(0, 4, finish, 0)
+    store = pltpu.make_async_copy(held, g_in, loc_sem.at[0])
+    store.start()
+    combine(DOWN)
+    relay(2)
+    turn(1)
+    leave(0)
+    relay(3)
+    turn(2)
+    leave(1)
+    relay(DOWN)
     turn(3)
     leave(2)
+    turn(DOWN)
     leave(3)
+    leave(DOWN)
 
     mine = lax.rem(z, 2)
     for s in range(8):
@@ -377,10 +374,11 @@
         total_d = total_d + zrd[s].astype(F32)
     whole = jnp.concatenate([total, pltpu.roll(total, 64, 1)[16:64]], axis=0)
     whole = jnp.where(x_odd, pltpu.roll(whole, 108, 0), whole)
-    g_conv[...] = whole[0:108, 0:64]
+    sums[0:112] = whole
     total_d = jnp.where(core == 1, pltpu.roll(total_d, 64, 1), total_d)
     total_d = jnp.where(x_odd, pltpu.roll(total_d, 12, 0), total_d)
-    g_down[...] = total_d[0:12, 0:64]
+    sums[112:128] = total_d
+    store.wait()
 
     for i in range(6):
         @pl.when(halo[i][3])
@@ -396,12 +394,20 @@
             z_wait(ztd.at[c], zrd, zsd.at[c, k], zrds, 2 * c + core, k)
 
 
+def hand_out(given, sums, g_in, g_conv, g_down):
+    g_in[...] = given[...]
+    g_conv[...] = sums[0:112].T[0:64, 0:108]
+    g_down[...] = sums[112:124, 0:64]
+
+
 def body(clip, weight, down, gout):
     vmem = pltpu.VMEM
     chunk = []
     for n in SIZES:
         full, pair = (4, 4, n, 128), (2, 2, n, 128)
-        chunk += [vmem(s, BF16) for s in (full, full, full, pair, pair, pair, pair, (4, n, 128), (3, n, 128))]
+        chunk += [vmem(s, BF16) for s in (full, full, full, pair, pair, pair, pair)]
+        later = BF16 if n == 112 else F32
+        chunk += [vmem((4, n, 128), later), vmem((3, n, 128), later)]
     dma = pltpu.SemaphoreType.DMA
     scratch = [
         vmem((3, 3, 3, CH, CH), BF16),
@@ -415,10 +421,11 @@
         vmem((4 * COLS, CH), F32),
         vmem((27 * CH, CH), F32),
         vmem((3 * CH, CH), F32),
+        vmem((4, 1, COLS, CH), BF16),
         vmem((4, 2, 64, 128), BF16),
-        vmem((4, 16, 128), BF16),
+        vmem((4, 16, 128), F32),
         vmem((8, 64, 128), BF16),
-        vmem((8, 16, 128), BF16),
+        vmem((8, 16, 128), F32),
         *chunk,
         dma((6,)),
         dma((6,)),
@@ -430,19 +437,27 @@
         dma((8,)),
         dma((8,)),
     ]
-    return pl.pallas_call(
+    g_in, sums = pl.pallas_call(
         kernel,
-        out_shape=(
-            jax.ShapeDtypeStruct(clip.shape, BF16),
-            jax.ShapeDtypeStruct((108, 64), F32),
-            jax.ShapeDtypeStruct((12, 64), F32),
-        ),
+        out_shape=(jax.ShapeDtypeStruct(clip.shape, BF16), jax.ShapeDtypeStruct((128, 128), F32)),
         in_specs=[pl.BlockSpec(memory_space=pl.ANY)] * 4,
-        out_specs=[pl.BlockSpec(memory_space=vmem)] * 3,
+        out_specs=[pl.BlockSpec(memory_space=pl.ANY), pl.BlockSpec(memory_space=vmem)],
         scratch_shapes=scratch,
         compiler_params=pltpu.CompilerParams(collective_id=0, has_side_effects=True),
         name="block_backward",
     )(clip, weight, down, gout)
+    g_in, g_conv, g_down = pl.pallas_call(
+        hand_out,
+        out_shape=(
+            jax.ShapeDtypeStruct(clip.shape, BF16),
+            jax.ShapeDtypeStruct((64, 108), F32),
+            jax.ShapeDtypeStruct((12, 64), F32),
+        ),
+        in_specs=[pl.BlockSpec(memory_space=vmem)] * 2,
+        out_specs=[pl.BlockSpec(memory_space=vmem)] * 3,
+        name="hand_out",
+    )(g_in, sums)
+    return g_in, g_conv.T, g_down
 
 
 def solution(mesh):

time: 56.7 us -> 55.4 us (0.977)
  the two profiles are of different devices: /device:TPU:4 before, /device:TPU:1 now
where the time goes in v2:
time: 55.4 us; the launch traced here: 55.3 us
  Pallas kernels  54.6 us (99%)
  between operations  0.64 us (1%)
    pallas_call x1, Pallas kernels, body(): pl.pallas_call(kernel, out_shape=(jax.ShapeDtypeStruct(clip.shape, BF16),...  53 us
    pallas_call x1, Pallas kernels, body(): pl.pallas_call(hand_out, out_shape=(jax.ShapeDtypeStruct(clip.shape, BF16...  1.68 us

profile of v2, /device:TPU:1, one launch (start us, length us, event | category | flops | bytes accessed | tf_op | source)
XLA Modules:
  0.0 55.3 jit_solution(1396490446148632536)
XLA Ops:
  0.6 53.0 %block_backward.1 = (bf16[4,1,128,256]{3,2,1,0:T(8,128)(2,1)}, f32[128,128]{1,0:T(8,128)}) custom-call(bf16[4,1,128,256]{3,2,1,0:T(8,128)(2,1)} %clip.1, bf16[3,3,3,256,256]{4,3,2,1,0:T(8,128)(2,1)} %weight.1, bf16[3,256,256]{2,1,0:T(8,128)(2,1)} %down.1, bf16[2,1,128,256]{3,2,1,0:T(8,128)(2,1)} %gout.1), custom_call_target="tpu_custom_call" | custom-call | tf_op jit(solution)/shard_map/block_backward/pallas_call | solution.py:440
  53.6 1.7 %hand_out.1 = (bf16[4,1,128,256]{3,2,1,0:T(8,128)(2,1)}, f32[64,108]{1,0:T(8,128)}, f32[12,64]{1,0:T(8,128)}) custom-call(bf16[4,1,128,256]{3,2,1,0:T(8,128)(2,1)} %get-tuple-element.8.given, f32[128,128]{1,0:T(8,128)} %get-tuple-element.9.sums), custom_call_target="tpu_custom_call" | custom-call | tf_op jit(solution)/shard_map/hand_out/pallas_call | solution.py:449

commit v3 on v2

--- a/solution.py
+++ b/solution.py
@@ -88,11 +88,16 @@
     halo = [
         (gout.at[:, 0], go.at[0, pl.ds(0, 2)], near(0, 1), h < 63, h > 0),
         (gout.at[:, 0], go.at[2, pl.ds(0, 2)], near(0, -1), h > 0, h < 63),
-        (gout.at[:, 0], go.at[0, pl.ds(2, 2)], near(-1, 1), (tm > 0) & (h < 63), (tm < 3) & (h > 0)),
-        (gout.at[:, 0], go.at[2, pl.ds(2, 2)], near(-1, -1), (tm > 0) & (h > 0), (tm < 3) & (h < 63)),
-        (gout.at[:, 0], go.at[1, pl.ds(2, 2)], near(-1, 0), tm > 0, tm < 3),
         (clip.at[pl.ds(2, 2), 0], cl.at[pl.ds(0, 2)], near(1, 0), tm < 3, tm > 0),
     ]
+    for frame in range(2):
+        late = gout.at[pl.ds(frame, 1), 0]
+        place = pl.ds(2 + frame, 1)
+        halo += [
+            (late, go.at[1, place], near(-1, 0), tm > 0, tm < 3),
+            (late, go.at[0, place], near(-1, 1), (tm > 0) & (h < 63), (tm < 3) & (h > 0)),
+            (late, go.at[2, place], near(-1, -1), (tm > 0) & (h > 0), (tm < 3) & (h < 63)),
+        ]
     copies = [remote(s, d, halo_s.at[i], halo_r.at[i], to) for i, (s, d, to, _, _) in enumerate(halo)]
 
     def when_start(i):
@@ -110,7 +115,7 @@
             dst = halo[i][1]
             dst[...] = jnp.zeros(dst.shape, BF16)
 
-    for i in (5, 0, 1, 4, 2, 3):
+    for i in (3, 2, 4, 5, 0, 1, 6, 7, 8):
         when_start(i)
 
     row = lax.broadcasted_iota(jnp.int32, (COLS, CH), 0)
@@ -122,16 +127,11 @@
         acts[0, f] = before.astype(BF16)
         acts[1, f] = act.astype(BF16)
         acts[2, f] = after.astype(BF16)
+        act_t[f] = act.T.astype(BF16)
         return carry
 
     loads[0].wait()
     lax.fori_loop(2, 6, act_frame, 0)
-    act_t[...] = acts[1, pl.ds(2, 4)].reshape(4 * COLS, CH).T
-    when_recv(5)
-    lax.fori_loop(0, 2, act_frame, 0)
-    for a in range(3):
-        loads[3 + a].wait()
-
     def conv_rows(b, carry):
         total = jnp.zeros((4 * COLS, CH), F32)
         for a in range(3):
@@ -142,20 +142,29 @@
         cb[b] = total.astype(BF16).reshape(4, COLS, CH)
         return carry
 
-    lax.fori_loop(0, 3, conv_rows, 0)
-
     def grad_rows(r):
-        later = go[r, pl.ds(1, 3)].reshape(3 * COLS, CH)
-        here = go[r, pl.ds(0, 3)].reshape(3 * COLS, CH)
+        later = go[r, pl.ds(1, 2)].reshape(2 * COLS, CH)
+        here = go[r, pl.ds(0, 2)].reshape(2 * COLS, CH)
         even = nt(later, dwn[0]) + nt(here, dwn[2])
         odd = nt(later, dwn[1])
-        for v in range(3):
-            for k, whole in ((0, even), (1, odd)):
-                value = whole[v * COLS : (v + 1) * COLS]
-                before, after = shifted(value, row)
-                gs[0, r, 2 * v + k] = after.astype(BF16)
-                gs[1, r, 2 * v + k] = value.astype(BF16)
-                gs[2, r, 2 * v + k] = before.astype(BF16)
+        for v in range(2):
+            place(r, 2 * v, even[v * COLS : (v + 1) * COLS])
+            place(r, 2 * v + 1, odd[v * COLS : (v + 1) * COLS])
+
+    def place(r, f, value):
+        before, after = shifted(value, row)
+        gs[0, r, f] = after.astype(BF16)
+        gs[1, r, f] = value.astype(BF16)
+        gs[2, r, f] = before.astype(BF16)
+
+    def grad_tail():
+        later = jnp.concatenate([go[r, 3] for r in range(3)], axis=0)
+        here = jnp.concatenate([go[r, 2] for r in range(3)], axis=0)
+        even = nt(later, dwn[0]) + nt(here, dwn[2])
+        odd = nt(later, dwn[1])
+        for r in range(3):
+            place(r, 4, even[r * COLS : (r + 1) * COLS])
+            place(r, 5, odd[r * COLS : (r + 1) * COLS])
 
     def down_terms():
         for k, pairs in ((0, ((0, 1), (2, 2))), (1, ((1, 1), (3, 2))), (2, ((0, 0), (2, 1)))):
@@ -169,9 +178,10 @@
         def one(i, carry):
             ab = start + step * i
             a, b = lax.div(ab, 3), lax.rem(ab, 3)
+            lhs = jnp.concatenate([act_t[a + f] for f in range(4)], axis=1)
             for s in range(3):
-                rhs = gs[s, 2 - b, pl.ds(2 - a, 4)].reshape(4 * COLS, CH)
-                part[pl.ds(pl.multiple_of((3 * ab + s) * CH, CH), CH), :] = nn(act_t[...], rhs)
+                rhs = gs[s, 2 - b, pl.ds(0, 4)].reshape(4 * COLS, CH)
+                part[pl.ds(pl.multiple_of((3 * ab + s) * CH, CH), CH), :] = nn(lhs, rhs)
             return carry
 
         lax.fori_loop(0, count, one, 0)
@@ -319,12 +329,14 @@
 
     loads[1].wait()
     loads[2].wait()
-    when_recv(4)
+    when_recv(3)
     grad_rows(1)
+    when_recv(2)
+    lax.fori_loop(0, 2, act_frame, 0)
     taps(*OWN_ROW)
-    acc[...] = grad_act(1, jnp.zeros(acc.shape, F32))
-
-    for i in range(4):
+    for a in range(3):
+        loads[3 + a].wait()
+    for i in (0, 1, 4, 5):
         when_recv(i)
     grad_rows(0)
     grad_rows(2)
@@ -332,30 +344,36 @@
         taps(*TAPS[c])
         hand_over(c)
     combine(0)
+    combine(1)
+    combine(2)
+    combine(3)
+    lax.fori_loop(0, 3, conv_rows, 0)
+    relay(0)
+    when_recv(6)
+    when_recv(7)
+    when_recv(8)
     down_terms()
     hand_over(DOWN)
-    combine(1)
-    acc[...] = grad_act(0, acc[...])
-    relay(0)
-    combine(2)
+    grad_tail()
+    relay(1)
+    combine(DOWN)
+    relay(2)
+    acc[...] = grad_act(0, jnp.zeros(acc.shape, F32))
+    relay(3)
+    turn(0)
+    acc[...] = grad_act(1, acc[...])
+    relay(DOWN)
+    turn(1)
     acc[...] = grad_act(2, acc[...])
-    relay(1)
-    combine(3)
-    turn(0)
+    turn(2)
+    leave(0)
     lax.fori_loop(0, 4, finish, 0)
     store = pltpu.make_async_copy(held, g_in, loc_sem.at[0])
     store.start()
-    combine(DOWN)
-    relay(2)
-    turn(1)
-    leave(0)
-    relay(3)
-    turn(2)
+    turn(3)
     leave(1)
-    relay(DOWN)
-    turn(3)
+    turn(DOWN)
     leave(2)
-    turn(DOWN)
     leave(3)
     leave(DOWN)
 
@@ -380,7 +398,7 @@
     sums[112:128] = total_d
     store.wait()
 
-    for i in range(6):
+    for i in range(9):
         @pl.when(halo[i][3])
         def _():
             copies[i].wait_send()
@@ -415,7 +433,7 @@
         vmem((6, COLS, CH), BF16),
         vmem((3, 4, COLS, CH), BF16),
         vmem((3, 6, COLS, CH), BF16),
-        vmem((CH, 4 * COLS), BF16),
+        vmem((6, CH, COLS), BF16),
         vmem((3, 3, 6, COLS, CH), BF16),
         vmem((3, 4, COLS, CH), BF16),
         vmem((4 * COLS, CH), F32),
@@ -428,8 +446,8 @@
         vmem((8, 16, 128), F32),
         *chunk,
         dma((6,)),
-        dma((6,)),
-        dma((6,)),
+        dma((9,)),
+        dma((9,)),
         dma((5, 10)),
         dma((5, 10)),
         dma((4, 2)),

time: 55.4 us -> 50.4 us (0.910)
  Pallas kernels: 54.6 us -> 49.7 us
    pallas_call x1, Pallas kernels: 53 us -> 48 us  [body(): pl.pallas_call(kernel, out_shape=(jax.ShapeDtypeStruct(clip.shape, BF16),...]
where the time goes in v3:
time: 50.4 us; the launch traced here: 50.3 us
  Pallas kernels  49.7 us (99%)
  between operations  0.64 us (1%)
    pallas_call x1, Pallas kernels, body(): pl.pallas_call(kernel, out_shape=(jax.ShapeDtypeStruct(clip.shape, BF16),...  48 us
    pallas_call x1, Pallas kernels, body(): pl.pallas_call(hand_out, out_shape=(jax.ShapeDtypeStruct(clip.shape, BF16...  1.68 us

profile of v3, /device:TPU:1, one launch (start us, length us, event | category | flops | bytes accessed | tf_op | source)
XLA Modules:
  0.0 50.3 jit_solution(9983717986968835843)
XLA Ops:
  0.6 48.0 %block_backward.1 = (bf16[4,1,128,256]{3,2,1,0:T(8,128)(2,1)}, f32[128,128]{1,0:T(8,128)}) custom-call(bf16[4,1,128,256]{3,2,1,0:T(8,128)(2,1)} %clip.1, bf16[3,3,3,256,256]{4,3,2,1,0:T(8,128)(2,1)} %weight.1, bf16[3,256,256]{2,1,0:T(8,128)(2,1)} %down.1, bf16[2,1,128,256]{3,2,1,0:T(8,128)(2,1)} %gout.1), custom_call_target="tpu_custom_call" | custom-call | tf_op jit(solution)/shard_map/block_backward/pallas_call | solution.py:458
  48.7 1.7 %hand_out.1 = (bf16[4,1,128,256]{3,2,1,0:T(8,128)(2,1)}, f32[64,108]{1,0:T(8,128)}, f32[12,64]{1,0:T(8,128)}) custom-call(bf16[4,1,128,256]{3,2,1,0:T(8,128)(2,1)} %get-tuple-element.8.given, f32[128,128]{1,0:T(8,128)} %get-tuple-element.9.sums), custom_call_target="tpu_custom_call" | custom-call | tf_op jit(solution)/shard_map/hand_out/pallas_call | solution.py:467

commit v4 on v3

--- a/solution.py
+++ b/solution.py
@@ -40,7 +40,7 @@
     (wgt, dwn, cl, go, acts, act_t, gs, cb, acc, part, part_d, held) = take(12)
     (zt, ztd, zr, zrd) = take(4)
     bufs = [take(9) for _ in SIZES]
-    (loc_sem, halo_s, halo_r, red_s, red_r, zs, zsd, zrs, zrds) = take(9)
+    (loc_sem, halo_s, halo_r, red_s, red_r, zs, zsd, zrs, zrds, up, low) = take(11)
 
     tm = lax.axis_index("tm")
     h = lax.axis_index("height")
@@ -69,11 +69,20 @@
         )
 
     barrier = pltpu.get_barrier_semaphore()
-    peers = [near(dt, dh) for dt in (-1, 1) for dh in (-1, 0, 1)] + [near(0, -1), near(0, 1)]
-    peers += [first(d) for d in (1, 2, 3)] + [second(d) for d in (1, 2, 3)]
-    peers += [dev(x, y, lax.rem(z + d, 8), c) for d in range(1, 8) for c in (0, 1)]
-    for peer in peers:
+    ring = [first(d) for d in (1, 2, 3)] + [second(d) for d in (1, 2, 3)]
+    ring += [dev(x, y, lax.rem(z + d, 8), core) for d in (1, 7)]
+    for peer in ring:
         pl.semaphore_signal(barrier, inc=1, device_id=peer, device_id_type=MESH)
+    has_h = {-1: lax.div(h + 62, 63), 0: 1, 1: lax.div(125 - h, 63)}
+    has_t = {-1: lax.div(tm + 2, 3), 0: 1, 1: lax.div(5 - tm, 3)}
+    expected = len(ring)
+    for dt, dh in ((-1, 0), (1, 0), (0, -1), (0, 1), (-1, -1), (-1, 1), (1, -1), (1, 1)):
+        there = has_t[dt] * has_h[dh]
+        expected = expected + there
+
+        @pl.when(there == 1)
+        def _():
+            pl.semaphore_signal(barrier, inc=1, device_id=near(dt, dh), device_id_type=MESH)
 
     loads = [
         pltpu.make_async_copy(clip.at[:, 0], cl.at[pl.ds(2, 4)], loc_sem.at[0]),
@@ -83,7 +92,21 @@
     for load in loads:
         load.start()
 
-    pl.semaphore_wait(barrier, len(peers))
+    pl.semaphore_wait(barrier, expected)
+
+    above, below = dev(x, y, lax.rem(z + 1, 8), core), dev(x, y, lax.rem(z + 7, 8), core)
+
+    def tell(level):
+        pl.semaphore_signal(up.at[level], inc=1, device_id=below, device_id_type=MESH)
+        if level < 3:
+            pl.semaphore_signal(low.at[level], inc=1, device_id=above, device_id_type=MESH)
+
+    def hear(level):
+        pl.semaphore_wait(up.at[level], 1)
+        if level < 3:
+            pl.semaphore_wait(low.at[level], 1)
+
+    tell(0)
 
     halo = [
         (gout.at[:, 0], go.at[0, pl.ds(0, 2)], near(0, 1), h < 63, h > 0),
@@ -115,7 +138,7 @@
             dst = halo[i][1]
             dst[...] = jnp.zeros(dst.shape, BF16)
 
-    for i in (3, 2, 4, 5, 0, 1, 6, 7, 8):
+    for i in (3, 2, 4, 5, 0, 1):
         when_start(i)
 
     row = lax.broadcasted_iota(jnp.int32, (COLS, CH), 0)
@@ -327,55 +350,89 @@
         held[f, 0] = (gs[1, 1, f].astype(F32) + grad * (sig * (1.0 + value * (1.0 - sig)))).astype(BF16)
         return carry
 
+    for a in range(3):
+        loads[3 + a].wait()
+
+    def convolve():
+        lax.fori_loop(0, 3, conv_rows, 0)
+
+    def earlier():
+        when_recv(2)
+        lax.fori_loop(0, 2, act_frame, 0)
+
+    @pl.when(tm != 2)
+    def _():
+        earlier()
+        convolve()
+
     loads[1].wait()
     loads[2].wait()
     when_recv(3)
     grad_rows(1)
-    when_recv(2)
-    lax.fori_loop(0, 2, act_frame, 0)
+
+    @pl.when(tm == 2)
+    def _():
+        earlier()
+
     taps(*OWN_ROW)
-    for a in range(3):
-        loads[3 + a].wait()
+    hear(0)
+    tell(1)
+
+    @pl.when(tm == 2)
+    def _():
+        convolve()
+
     for i in (0, 1, 4, 5):
         when_recv(i)
+    for i in (6, 7, 8):
+        when_start(i)
     grad_rows(0)
     grad_rows(2)
-    for c in range(4):
-        taps(*TAPS[c])
-        hand_over(c)
+    taps(*TAPS[0])
+    hand_over(0)
+    taps(*TAPS[1])
+    hand_over(1)
     combine(0)
+    taps(*TAPS[2])
+    hand_over(2)
     combine(1)
+    taps(*TAPS[3])
+    hand_over(3)
+    down_terms()
+    hand_over(DOWN)
     combine(2)
     combine(3)
-    lax.fori_loop(0, 3, conv_rows, 0)
+    hear(1)
+    tell(2)
     relay(0)
-    when_recv(6)
-    when_recv(7)
-    when_recv(8)
-    down_terms()
-    hand_over(DOWN)
+    combine(DOWN)
+    relay(1)
+    relay(2)
+    relay(3)
+    relay(DOWN)
+    hear(2)
+    tell(3)
+    turn(0)
+    turn(1)
+    acc[...] = jnp.zeros(acc.shape, F32)
+    for i in (6, 7, 8):
+        when_recv(i)
     grad_tail()
-    relay(1)
-    combine(DOWN)
-    relay(2)
-    acc[...] = grad_act(0, jnp.zeros(acc.shape, F32))
-    relay(3)
-    turn(0)
+    acc[...] = grad_act(0, acc[...])
+    turn(2)
+    turn(3)
+    turn(DOWN)
     acc[...] = grad_act(1, acc[...])
-    relay(DOWN)
-    turn(1)
     acc[...] = grad_act(2, acc[...])
-    turn(2)
+    hear(3)
     leave(0)
+    leave(1)
+    leave(2)
+    leave(3)
+    leave(DOWN)
     lax.fori_loop(0, 4, finish, 0)
     store = pltpu.make_async_copy(held, g_in, loc_sem.at[0])
     store.start()
-    turn(3)
-    leave(1)
-    turn(DOWN)
-    leave(2)
-    leave(3)
-    leave(DOWN)
 
     mine = lax.rem(z, 2)
     for s in range(8):
@@ -454,6 +511,8 @@
         dma((4, 2)),
         dma((8,)),
         dma((8,)),
+        pltpu.SemaphoreType.REGULAR((4,)),
+        pltpu.SemaphoreType.REGULAR((3,)),
     ]
     g_in, sums = pl.pallas_call(
         kernel,

time: 50.4 us -> 48.5 us (0.962)
  Pallas kernels: 49.7 us -> 47.8 us
    pallas_call x1, Pallas kernels: 48 us -> 46.1 us  [body(): pl.pallas_call(kernel, out_shape=(jax.ShapeDtypeStruct(clip.shape, BF16),...]
where the time goes in v4:
time: 48.5 us; the launch traced here: 48.4 us
  Pallas kernels  47.8 us (99%)
  between operations  0.64 us (1%)
    pallas_call x1, Pallas kernels, body(): pl.pallas_call(kernel, out_shape=(jax.ShapeDtypeStruct(clip.shape, BF16),...  46.1 us
    pallas_call x1, Pallas kernels, body(): pl.pallas_call(hand_out, out_shape=(jax.ShapeDtypeStruct(clip.shape, BF16...  1.68 us

profile of v4, /device:TPU:1, one launch (start us, length us, event | category | flops | bytes accessed | tf_op | source)
XLA Modules:
  0.0 48.4 jit_solution(18336808862565359634)
XLA Ops:
  0.6 46.1 %block_backward.1 = (bf16[4,1,128,256]{3,2,1,0:T(8,128)(2,1)}, f32[128,128]{1,0:T(8,128)}) custom-call(bf16[4,1,128,256]{3,2,1,0:T(8,128)(2,1)} %clip.1, bf16[3,3,3,256,256]{4,3,2,1,0:T(8,128)(2,1)} %weight.1, bf16[3,256,256]{2,1,0:T(8,128)(2,1)} %down.1, bf16[2,1,128,256]{3,2,1,0:T(8,128)(2,1)} %gout.1), custom_call_target="tpu_custom_call" | custom-call | tf_op jit(solution)/shard_map/block_backward/pallas_call | solution.py:517
  46.8 1.7 %hand_out.1 = (bf16[4,1,128,256]{3,2,1,0:T(8,128)(2,1)}, f32[64,108]{1,0:T(8,128)}, f32[12,64]{1,0:T(8,128)}) custom-call(bf16[4,1,128,256]{3,2,1,0:T(8,128)(2,1)} %get-tuple-element.8.given, f32[128,128]{1,0:T(8,128)} %get-tuple-element.9.sums), custom_call_target="tpu_custom_call" | custom-call | tf_op jit(solution)/shard_map/hand_out/pallas_call | solution.py:526

commit v5 on v4

--- a/solution.py
+++ b/solution.py
@@ -113,14 +113,20 @@
         (gout.at[:, 0], go.at[2, pl.ds(0, 2)], near(0, -1), h > 0, h < 63),
         (clip.at[pl.ds(2, 2), 0], cl.at[pl.ds(0, 2)], near(1, 0), tm < 3, tm > 0),
     ]
+    odd, even = lax.rem(tm, 2) == 1, lax.rem(tm, 2) == 0
     for frame in range(2):
         late = gout.at[pl.ds(frame, 1), 0]
         place = pl.ds(2 + frame, 1)
+        sends, takes = (tm > 0, tm < 3) if frame == 0 else (tm == 2, tm == 1)
         halo += [
             (late, go.at[1, place], near(-1, 0), tm > 0, tm < 3),
-            (late, go.at[0, place], near(-1, 1), (tm > 0) & (h < 63), (tm < 3) & (h > 0)),
-            (late, go.at[2, place], near(-1, -1), (tm > 0) & (h > 0), (tm < 3) & (h < 63)),
+            (late, go.at[0, place], near(-1, 1), sends & (h < 63), takes & (h > 0)),
+            (late, go.at[2, place], near(-1, -1), sends & (h > 0), takes & (h < 63)),
         ]
+    halo += [
+        (go.at[0, pl.ds(1, 1)], go.at[0, pl.ds(3, 1)], near(-1, 0), odd & (h > 0), even & (h > 0)),
+        (go.at[2, pl.ds(1, 1)], go.at[2, pl.ds(3, 1)], near(-1, 0), odd & (h < 63), even & (h < 63)),
+    ]
     copies = [remote(s, d, halo_s.at[i], halo_r.at[i], to) for i, (s, d, to, _, _) in enumerate(halo)]
 
     def when_start(i):
@@ -137,6 +143,16 @@
         def _():
             dst = halo[i][1]
             dst[...] = jnp.zeros(dst.shape, BF16)
+
+    def late_rows(r, there, direct, passed):
+        for i in (direct, passed):
+            @pl.when(halo[i][4])
+            def _():
+                copies[i].wait_recv()
+
+        @pl.when(jnp.logical_not(there & (tm < 3)))
+        def _():
+            go[r, 3] = jnp.zeros((COLS, CH), BF16)
 
     for i in (3, 2, 4, 5, 0, 1):
         when_start(i)
@@ -347,7 +363,7 @@
         value = cl[f + 2].astype(F32)
         sig = sigmoid(value)
         grad = acc[pl.ds(pl.multiple_of(f * COLS, COLS), COLS), :]
-        held[f, 0] = (gs[1, 1, f].astype(F32) + grad * (sig * (1.0 + value * (1.0 - sig)))).astype(BF16)
+        g_in[f, 0] = (gs[1, 1, f].astype(F32) + grad * (sig * (1.0 + value * (1.0 - sig)))).astype(BF16)
         return carry
 
     for a in range(3):
@@ -384,7 +400,7 @@
 
     for i in (0, 1, 4, 5):
         when_recv(i)
-    for i in (6, 7, 8):
+    for i in (6, 7, 8, 9, 10):
         when_start(i)
     grad_rows(0)
     grad_rows(2)
@@ -415,8 +431,9 @@
     turn(0)
     turn(1)
     acc[...] = jnp.zeros(acc.shape, F32)
-    for i in (6, 7, 8):
-        when_recv(i)
+    when_recv(6)
+    late_rows(0, h > 0, 7, 9)
+    late_rows(2, h < 63, 8, 10)
     grad_tail()
     acc[...] = grad_act(0, acc[...])
     turn(2)
@@ -431,8 +448,6 @@
     leave(3)
     leave(DOWN)
     lax.fori_loop(0, 4, finish, 0)
-    store = pltpu.make_async_copy(held, g_in, loc_sem.at[0])
-    store.start()
 
     mine = lax.rem(z, 2)
     for s in range(8):
@@ -453,9 +468,8 @@
     total_d = jnp.where(core == 1, pltpu.roll(total_d, 64, 1), total_d)
     total_d = jnp.where(x_odd, pltpu.roll(total_d, 12, 0), total_d)
     sums[112:128] = total_d
-    store.wait()
-
-    for i in range(9):
+
+    for i in range(11):
         @pl.when(halo[i][3])
         def _():
             copies[i].wait_send()
@@ -503,8 +517,8 @@
         vmem((8, 16, 128), F32),
         *chunk,
         dma((6,)),
-        dma((9,)),
-        dma((9,)),
+        dma((11,)),
+        dma((11,)),
         dma((5, 10)),
         dma((5, 10)),
         dma((4, 2)),
@@ -516,9 +530,9 @@
     ]
     g_in, sums = pl.pallas_call(
         kernel,
-        out_shape=(jax.ShapeDtypeStruct(clip.shape, BF16), jax.ShapeDtypeStruct((128, 128), F32)),
+        out_shape=(vmem(clip.shape, BF16), vmem((128, 128), F32)),
         in_specs=[pl.BlockSpec(memory_space=pl.ANY)] * 4,
-        out_specs=[pl.BlockSpec(memory_space=pl.ANY), pl.BlockSpec(memory_space=vmem)],
+        out_specs=[pl.BlockSpec(memory_space=vmem), pl.BlockSpec(memory_space=vmem)],
         scratch_shapes=scratch,
         compiler_params=pltpu.CompilerParams(collective_id=0, has_side_effects=True),
         name="block_backward",
@@ -533,7 +547,7 @@
         in_specs=[pl.BlockSpec(memory_space=vmem)] * 2,
         out_specs=[pl.BlockSpec(memory_space=vmem)] * 3,
         name="hand_out",
-    )(g_in, sums)
+    )(pltpu.with_memory_space_constraint(g_in, vmem), pltpu.with_memory_space_constraint(sums, vmem))
     return g_in, g_conv.T, g_down
 
 

time: 48.5 us -> 46.7 us (0.963)
  Pallas kernels: 47.8 us -> 46 us
    pallas_call x1, Pallas kernels: 1.68 us -> 0.73 us  [body(): pl.pallas_call(hand_out, out_shape=(jax.ShapeDtypeStruct(clip.shape, BF16...]
    pallas_call x1, Pallas kernels: 46.1 us -> 45.3 us  [body(): pl.pallas_call(kernel, out_shape=(vmem(clip.shape, BF16), vmem((128, 128)...]
where the time goes in v5:
time: 46.7 us; the launch traced here: 46.6 us
  Pallas kernels  46 us (99%)
  between operations  0.64 us (1%)
    pallas_call x1, Pallas kernels, body(): pl.pallas_call(kernel, out_shape=(vmem(clip.shape, BF16), vmem((128, 128)...  45.3 us

profile of v5, /device:TPU:1, one launch (start us, length us, event | category | flops | bytes accessed | tf_op | source)
XLA Modules:
  0.0 46.6 jit_solution(9059817110797674829)
XLA Ops:
  0.6 45.3 %block_backward.1 = (bf16[4,1,128,256]{3,2,1,0:T(8,128)(2,1)S(1)}, f32[128,128]{1,0:T(8,128)S(1)}) custom-call(bf16[4,1,128,256]{3,2,1,0:T(8,128)(2,1)} %clip.1, bf16[3,3,3,256,256]{4,3,2,1,0:T(8,128)(2,1)} %weight.1, bf16[3,256,256]{2,1,0:T(8,128)(2,1)} %down.1, bf16[2,1,128,256]{3,2,1,0:T(8,128)(2,1)} %gout.1), custom_call_target="tpu_custom_call" | custom-call | tf_op jit(solution)/shard_map/block_backward/pallas_call | solution.py:531
  45.9 0.7 %hand_out.1 = (bf16[4,1,128,256]{3,2,1,0:T(8,128)(2,1)}, f32[64,108]{1,0:T(8,128)}, f32[12,64]{1,0:T(8,128)}) custom-call(bf16[4,1,128,256]{3,2,1,0:T(8,128)(2,1)S(1)} %get-tuple-element.8.given, f32[128,128]{1,0:T(8,128)S(1)} %get-tuple-element.9.sums), custom_call_target="tpu_custom_call" | custom-call | tf_op jit(solution)/shard_map/hand_out/pallas_call | solution.py:540

commit v6 on v5

--- a/solution.py
+++ b/solution.py
@@ -13,7 +13,8 @@
 SIZES = (112, 112, 112, 112, 64)
 DOWN = 4
 OWN_ROW = (1, 3, 3)
-TAPS = ((0, 5, 2), (2, 4, 2), (3, 0, 1), (8, 0, 1))
+ROW_ABOVE = (2, 3, 3)
+TAPS = ((0, 0, 1), (6, 0, 1), (3, 0, 1))
 
 
 def nt(lhs, rhs):
@@ -398,11 +399,14 @@
     def _():
         convolve()
 
-    for i in (0, 1, 4, 5):
+    for i in (0, 4):
+        when_recv(i)
+    grad_rows(0)
+    taps(*ROW_ABOVE)
+    for i in (1, 5):
         when_recv(i)
     for i in (6, 7, 8, 9, 10):
         when_start(i)
-    grad_rows(0)
     grad_rows(2)
     taps(*TAPS[0])
     hand_over(0)
@@ -412,7 +416,6 @@
     taps(*TAPS[2])
     hand_over(2)
     combine(1)
-    taps(*TAPS[3])
     hand_over(3)
     down_terms()
     hand_over(DOWN)

time: 46.7 us -> 47.7 us (1.021)
  Pallas kernels: 46 us -> 47 us
    pallas_call x1, Pallas kernels: 45.3 us -> 46.3 us  [body(): pl.pallas_call(kernel, out_shape=(vmem(clip.shape, BF16), vmem((128, 128)...]
where the time goes in v6:
time: 47.7 us
  Pallas kernels  47 us (99%)
  between operations  0.64 us (1%)
    pallas_call x1, Pallas kernels, body(): pl.pallas_call(kernel, out_shape=(vmem(clip.shape, BF16), vmem((128, 128)...  46.3 us

profile of v6, /device:TPU:1, one launch (start us, length us, event | category | flops | bytes accessed | tf_op | source)
XLA Modules:
  0.0 47.7 jit_solution(3729579313453907459)
XLA Ops:
  0.6 46.3 %block_backward.1 = (bf16[4,1,128,256]{3,2,1,0:T(8,128)(2,1)S(1)}, f32[128,128]{1,0:T(8,128)S(1)}) custom-call(bf16[4,1,128,256]{3,2,1,0:T(8,128)(2,1)} %clip.1, bf16[3,3,3,256,256]{4,3,2,1,0:T(8,128)(2,1)} %weight.1, bf16[3,256,256]{2,1,0:T(8,128)(2,1)} %down.1, bf16[2,1,128,256]{3,2,1,0:T(8,128)(2,1)} %gout.1), custom_call_target="tpu_custom_call" | custom-call | tf_op jit(solution)/shard_map/block_backward/pallas_call | solution.py:534
  46.9 0.7 %hand_out.1 = (bf16[4,1,128,256]{3,2,1,0:T(8,128)(2,1)}, f32[64,108]{1,0:T(8,128)}, f32[12,64]{1,0:T(8,128)}) custom-call(bf16[4,1,128,256]{3,2,1,0:T(8,128)(2,1)S(1)} %get-tuple-element.8.given, f32[128,128]{1,0:T(8,128)S(1)} %get-tuple-element.9.sums), custom_call_target="tpu_custom_call" | custom-call | tf_op jit(solution)/shard_map/hand_out/pallas_call | solution.py:543
